TPU v7x, 256 devices: a whole 4x4x8 slice. The times are simulated.
256 devices in a mesh: gx: 16 (over z, core), gy: 16 (over x, y).
Axes of the slice: x: 4, y: 4, z: 8, core: 2. Of those that a mesh axis runs over, the one named last changes fastest.
Arguments:
- features: bfloat16 [256, 256, 1, 1024], P('gx', 'gy'), may hold values from -6 to 6
- slot_map: int32 [16, 16, 2], replicated, may hold values from -1 to 0, as said below
- tap_weights: float32 [27, 64], replicated, may hold values from -1.25 to 1.25
- gain: float32 [64], replicated, may hold values from 0.5 to 1.5
- mix_weight: bfloat16 [64, 64], replicated, may hold values from -0.75 to 0.75
- cotangent: bfloat16 [256, 256, 1, 1024], P('gx', 'gy'), may hold values from -6 to 6
Outputs:
- mixed: bfloat16 [256, 256, 1, 1024], P('gx', 'gy')
- grad_features: bfloat16 [256, 256, 1, 1024], P('gx', 'gy')
- grad_taps: float32 [27, 64], replicated
- grad_gain: float32 [64], replicated
- grad_mix: float32 [64, 64], replicated
Inputs may be any that keep to these rules, and one draw needn't show every extreme that they name: `slot_map`: in each block column the active levels carry slot numbers 0, 1, 2, ... in increasing level order and the others carry -1; every block column has exactly 1 active block.
All inputs are finite; a program needn't handle non-finite values.
Results may differ from a plain program's by a relative error of at most 0.0039.
Values may be sent and summed in bfloat16 or wider, within the bound.
A program may use at most 128 MiB of HBM per device.

v0:
```python
import jax
import jax.numpy as jnp
from jax import lax
from jax.sharding import PartitionSpec as P

EPS = 1e-05


def extended_2(cells, sides, width):
    for axis, dim in sides:
        count = lax.axis_size(axis)
        ends = count - 1
        head = lax.slice_in_dim(cells, 0, width, axis=dim)
        tail = lax.slice_in_dim(cells, cells.shape[dim] - width, cells.shape[dim], axis=dim)
        cells = jnp.concatenate(
            [
                lax.ppermute(tail, axis, [(i, (i + 1) % count) for i in range(ends)]),
                cells,
                lax.ppermute(head, axis, [((i + 1) % count, i) for i in range(ends)]),
            ],
            axis=dim,
        )
    return cells


def one_hot_map(level_slots, slot_count):
    slot_ids = jnp.arange(slot_count, dtype=jnp.int32)
    return (level_slots[..., None] == slot_ids).astype(jnp.bfloat16)


def slot_lookup(center, slot_count):
    slot_ids = jnp.arange(slot_count, dtype=jnp.int32)
    matches = center[:, None] == slot_ids[None, :]
    level_ids = jnp.arange(center.shape[0], dtype=jnp.int32)[:, None]
    position = jnp.sum(jnp.where(matches, level_ids, 0), axis=0)
    active = jnp.any(matches, axis=0)
    return (position, active)


def slot_slabs(extended, position, active, channels):
    levels = extended.shape[2]
    level_pad = jnp.pad(extended, ((0, 0), (0, 0), (1, 1), (0, 0)))
    level_ids = jnp.arange(levels + 2, dtype=jnp.int32)
    wanted = position[:, None] + jnp.arange(3, dtype=jnp.int32)[None, :]
    select = (wanted[:, :, None] == level_ids[None, None, :]) & active[:, None, None]
    picked = jnp.einsum(
        "xypf,skp->xyskf",
        level_pad,
        select.astype(jnp.bfloat16),
        preferred_element_type=jnp.float32,
    ).astype(jnp.bfloat16)
    below = picked[:, :, :, 0, -channels:]
    middle = picked[:, :, :, 1, :]
    above = picked[:, :, :, 2, :channels]
    return jnp.concatenate([below, middle, above], axis=-1)


def stencil(padded, taps):
    channels = taps.shape[1]
    inner = padded.shape[0] - 2
    length = padded.shape[-1] - 2 * channels
    accum_sum = jnp.zeros((inner, inner) + padded.shape[2:-1] + (length,), jnp.float32)
    for tap_index in range(27):
        off_x = tap_index // 9
        off_y = tap_index // 3 % 3
        off_z = tap_index % 3
        shifted = padded[
            off_x : off_x + inner,
            off_y : off_y + inner,
            ...,
            channels * off_z : channels * off_z + length,
        ].astype(jnp.float32)
        accum_sum = accum_sum + shifted * jnp.tile(taps[tap_index], length // channels)
    return accum_sum


def tap_grads(padded, grads, channels):
    inner = padded.shape[0] - 2
    length = padded.shape[-1] - 2 * channels
    rows_out = []
    for tap_index in range(27):
        off_x = tap_index // 9
        off_y = tap_index // 3 % 3
        off_z = tap_index % 3
        shifted = padded[
            off_x : off_x + inner,
            off_y : off_y + inner,
            ...,
            channels * off_z : channels * off_z + length,
        ].astype(jnp.float32)
        rows_out.append(jnp.sum((shifted * grads).reshape(-1, channels), axis=0))
    return jnp.stack(rows_out)


def norm_forward(depth_slots):
    mean_square = jnp.mean(depth_slots * depth_slots, axis=-1, keepdims=True)
    inv_rms = lax.rsqrt(mean_square + EPS)
    return (depth_slots * inv_rms, inv_rms)


def norm_backward(grad_norm, normed, inv_rms, gain):
    grad_scaled = grad_norm * gain
    return inv_rms * (grad_scaled - normed * jnp.mean(grad_scaled * normed, axis=-1, keepdims=True))


def shards(features, slot_map, tap_weights, gain, mix_weight, cotangent):
    block_side = features.shape[0]
    slot_count = features.shape[2]
    lane_width = features.shape[3]
    channels = gain.shape[0]
    depth_cells = lane_width // channels
    levels = slot_map.shape[2]
    cell_shape = (block_side, block_side, slot_count, depth_cells, channels)
    grid_row = lax.axis_index("gx")
    grid_col = lax.axis_index("gy")
    padded_map = jnp.pad(slot_map, ((1, 1), (1, 1), (0, 0)), constant_values=-1)
    near_maps = lax.dynamic_slice(padded_map, (grid_row, grid_col, jnp.int32(0)), (3, 3, levels))
    center = near_maps[1, 1]
    position, active = slot_lookup(center, slot_count)
    keep_mask = active.astype(jnp.float32)[None, None, :, None, None]

    def extend(slot_data):
        dense_field = jnp.einsum(
            "xysf,ps->xypf",
            slot_data,
            one_hot_map(center, slot_count),
            preferred_element_type=jnp.float32,
        ).astype(jnp.bfloat16)
        extended = extended_2(dense_field, (("gx", 0), ("gy", 1)), 1)
        return slot_slabs(extended, position, active, channels)

    padded_in = extend(features)
    depth_slots = stencil(padded_in, tap_weights).reshape(cell_shape)
    normed, inv_rms = norm_forward(depth_slots)
    norm_bf = (normed * gain).astype(jnp.bfloat16)
    branch = jnp.einsum("xyszc,cd->xyszd", norm_bf, mix_weight, preferred_element_type=jnp.float32)
    mixed = (
        ((features.reshape(cell_shape).astype(jnp.float32) + branch) * keep_mask)
        .astype(jnp.bfloat16)
        .reshape(features.shape)
    )
    grad_out = cotangent.reshape(cell_shape) * keep_mask.astype(jnp.bfloat16)
    grad_mix_part = jnp.einsum(
        "xyszc,xyszd->cd", norm_bf, grad_out, preferred_element_type=jnp.float32
    )
    grad_norm = jnp.einsum(
        "xyszd,cd->xyszc", grad_out, mix_weight, preferred_element_type=jnp.float32
    )
    grad_gain_part = jnp.sum(grad_norm * normed, axis=(0, 1, 2, 3))
    grad_depth = (
        (norm_backward(grad_norm, normed, inv_rms, gain) * keep_mask)
        .astype(jnp.bfloat16)
        .reshape(features.shape)
    )
    padded_grad = extend(grad_depth)
    back_slots = stencil(padded_grad, tap_weights[::-1])
    grad_features = (
        ((cotangent.astype(jnp.float32) + back_slots).reshape(cell_shape) * keep_mask)
        .astype(jnp.bfloat16)
        .reshape(features.shape)
    )
    grad_center = padded_grad[1:-1, 1:-1, :, channels:-channels].astype(jnp.float32)
    grad_taps_part = tap_grads(padded_in, grad_center, channels)
    grad_taps, grad_mix, grad_gain = lax.psum(
        (grad_taps_part, grad_mix_part, grad_gain_part), ("gx", "gy")
    )
    return (mixed, grad_features, grad_taps, grad_gain, grad_mix)


def solution(mesh):
    return jax.shard_map(
        shards,
        mesh=mesh,
        in_specs=(P("gx", "gy", None, None), P(), P(), P(), P(), P("gx", "gy", None, None)),
        out_specs=(P("gx", "gy", None, None), P("gx", "gy", None, None), P(), P(), P()),
        check_vma=False,
    )
```

profile of v0, /device:TPU:1, one launch (start us, length us, event | category | flops | bytes accessed | tf_op | source)
XLA Modules:
  0.0 338.6 jit_solution(7447671005226463131)
XLA Ops:
  4.5 5.1 %collective-permute-start = (bf16[1,16,2,1024]{3,2,1,0:T(2,128)(2,1)S(1)}, bf16[1,16,2,1024]{3,2,1,0:T(2,128)(2,1)S(1)}, u32[]{:S(2)}, u32[]{:S(2)}) collective-permute-start(bf16[1,16,2,1024]{3,2,1,0:T(2,128)(2,1)S(1)} %get-tuple-element.75), channel_id=1, source_target_pairs={{0,16},{16,32},{32,48},{48,64},{64,80},{80,96},{96,112},{112,128},... | collective-permute-start | bytes 196616 | tf_op jit(solution)/shard_map/ppermute | solution.py:17
  19.4 3.2 collective-permute-start.2
  24.8 2.9 collective-permute-done.3
  27.8 4.5 %convert_bitcast_fusion.1 = bf16[18,18,1,3,1024]{4,3,1,0,2:T(4,128)(2,1)S(1)} fusion(bf16[18,1,2,1024]{3,2,1,0:T(2,128)(2,1)S(1)} %collective-permute-done.3, bf16[18,1,2,1024]{3,2,1,0:T(2,128)(2,1)S(1)} %collective-permute-done.2, bf16[1,16,2,1024]{3,2,1,0:T(2,128)(2,1)S(1)} %collective-permute-done.1, bf16[16,16,2,1024]{3,2,1,0:T(2,128)(2,1)S(1)} %fusion.52, ...), kind=kOutput, calls=%fused_computation.88 | convolution fusion | flops 32845848 | bytes 3317773 | tf_op jit(solution)/shard_map/xypf,skp->xyskf/dot_general | solution.py:46
  34.6 9.4 %fusion.125 = (f32[16,16,1,1024]{3,1,0,2:T(8,128)}, f32[16,16,1,1024]{3,1,0,2:T(8,128)}) fusion(f32[1024]{0:T(1024)S(1)} %mul.720, bf16[18,18,1,64]{3,1,0,2:T(8,128)(2,1)S(1)} %get-tuple-element.105, bf16[18,18,1,1024]{3,1,0,2:T(8,128)(2,1)S(1)} %bitcast.278, f32[1024]{0:T(1024)S(1)} %mul.717, f32[1024]{0:T(1024)S(1)} %mul.714, ...), kind=kLoop, calls=%fused_computation.308 | loop fusion | flops 35389440 | bytes 8032256 | tf_op jit(solution)/shard_map/mul | solution.py:96
  52.8 3.1 multiply_convert_fusion.2
  65.5 5.1 %collective-permute-start.4 = (bf16[1,16,2,1024]{3,2,1,0:T(2,128)(2,1)}, bf16[1,16,2,1024]{3,2,1,0:T(2,128)(2,1)}, u32[]{:S(2)}, u32[]{:S(2)}) collective-permute-start(bf16[1,16,2,1024]{3,2,1,0:T(2,128)(2,1)} %get-tuple-element.73), channel_id=1, source_target_pairs={{0,16},{16,32},{32,48},{48,64},{64,80},{80,96},{96,112},{112,128},... | collective-permute-start | bytes 196616 | tf_op jit(solution)/shard_map/ppermute | solution.py:17
  77.3 3.2 collective-permute-start.6
  83.5 3.0 reshape.456
  86.6 5.0 %convert_bitcast_fusion = bf16[18,18,1,3,1024]{4,3,1,0,2:T(4,128)(2,1)S(1)} fusion(bf16[18,1,2,1024]{3,2,1,0:T(2,128)(2,1)S(1)} %collective-permute-done.7, bf16[18,1,2,1024]{3,2,1,0:T(2,128)(2,1)S(1)} %collective-permute-done.6, bf16[1,16,2,1024]{3,2,1,0:T(2,128)(2,1)} %collective-permute-done.5, bf16[16,16,2,1024]{3,2,1,0:T(2,128)(2,1)S(1)} %fusion.54, ...), kind=kOutput, calls=%fused_computation.87 | convolution fusion | flops 32845848 | bytes 3317773 | tf_op jit(solution)/shard_map/xypf,skp->xyskf/dot_general | solution.py:46
  93.8 4.0 %convert_multiply_fusion.2 = (f32[16,16,1,1024]{3,1,0,2:T(8,128)}, f32[16,16,1,1024]{3,1,0,2:T(8,128)}, f32[16,16,1,1024]{3,1,0,2:T(8,128)}, f32[16,16,1,1024]{3...) fusion(bf16[18,18,1,1024]{3,1,0,2:T(8,128)(2,1)S(1)} %bitcast.279, ...), kind=kLoop, calls=%fused_computation.2 | loop fusion | flops 8126464 | bytes 7520768 | tf_op jit(solution)/shard_map/mul | solution.py:91
  97.7 4.4 %convert_multiply_fusion.3 = (f32[16,16,1,1024]{3,1,0,2:T(8,128)}, f32[16,16,1,1024]{3,1,0,2:T(8,128)}, f32[16,16,1,1024]{3,1,0,2:T(8,128)}, f32[16,16,1,1024]{3...) fusion(bf16[18,18,1,64]{3,1,0,2:T(8,128)(2,1)S(1)} %copy-done.10, ...), kind=kLoop, calls=%fused_computation.3 | loop fusion | flops 8126464 | bytes 7562240 | tf_op jit(solution)/shard_map/mul | solution.py:91
  102.2 4.3 %convert_multiply_fusion = (f32[16,16,1,1024]{3,1,0,2:T(8,128)}, f32[16,16,1,1024]{3,1,0,2:T(8,128)}, f32[16,16,1,1024]{3,1,0,2:T(8,128)}, f32[16,16,1,1024]{3,1...) fusion(bf16[18,18,1,64]{3,1,0,2:T(8,128)(2,1)S(1)} %copy-done.10, ...), kind=kLoop, calls=%fused_computation | loop fusion | flops 8126464 | bytes 7520768 | tf_op jit(solution)/shard_map/mul | solution.py:91
  106.4 4.0 %convert_multiply_fusion.1 = (f32[16,16,1,1024]{3,1,0,2:T(8,128)}, f32[16,16,1,1024]{3,1,0,2:T(8,128)}, f32[16,16,1,1024]{3,1,0,2:T(8,128)}, f32[16,16,1,1024]{3...) fusion(bf16[18,18,1,1024]{3,1,0,2:T(8,128)(2,1)S(1)} %bitcast.2, ...), kind=kLoop, calls=%fused_computation.1 | loop fusion | flops 4980736 | bytes 14680064 | tf_op jit(solution)/shard_map/mul | solution.py:91
  110.4 2.9 reshape.482
  115.4 2.8 reshape.458
  120.4 3.0 reshape.461
  125.6 2.8 reshape.464
  130.6 2.8 reshape.467
  135.6 2.8 reshape.470
  140.6 2.8 reshape.481
  155.6 2.8 reshape.476
  160.6 2.8 reshape.473
  165.6 2.8 reshape.479
  170.6 2.8 reshape.484
  185.5 3.1 reshape.466
  190.7 2.8 reshape.469
  205.7 2.8 reshape.480
  210.7 2.8 reshape.477
  215.7 2.8 reshape.474
  245.2 9.3 %fusion.106 = bf16[16,16,1,1024]{3,1,2,0:T(8,128)(2,1)} fusion(f32[]{:T(128)S(6)} %convert_element_type.307, f32[1024]{0:T(1024)S(1)} %copy-done.14, bf16[18,18,1,64]{3,1,0,2:T(8,128)(2,1)S(1)} %bitcast.290, bf16[18,18,1,1024]{3,1,0,2:T(8,128)(2,1)S(1)} %bitcast.287, f32[1024]{0:T(1024)S(1)} %mul.645, f32[1024]{0:T(1024)S(1)} %mul.648, ...), kind=kLoop, calls=%fused_computation.245 | loop fusion | flops 36175872 | bytes 6983684
  254.5 83.8 %all-reduce.3 = (f32[27,64]{1,0:T(8,128)}, f32[64]{0:T(128)}, f32[64,64]{1,0:T(8,128)}) all-reduce(f32[27,64]{1,0:T(8,128)S(1)} %stack.111, f32[64]{0:T(128)S(1)} %copy-done.54, f32[64,64]{1,0:T(8,128)S(1)} %convolution_bitcast_fusion), channel_id=1, replica_groups=mesh['gx'=16,'gy'=16] {'gx','gy'}, use_global_device_ids=true, to_apply=%region_31.32 | all-reduce | flops 5888 | bytes 47104 | tf_op jit(solution)/shard_map/psum | solution.py:164
  (258 shorter events, 135.9 us)
Async XLA Ops:
  0.6 52.2 %copy-start = (bf16[64,64]{1,0:T(8,128)(2,1)S(1)}, bf16[64,64]{1,0:T(8,128)(2,1)}, u32[]{:S(2)}) copy-start(bf16[64,64]{1,0:T(8,128)(2,1)} %param.10) | copy-start | bytes 24580
  4.4 12.5 %copy-start.7 = (bf16[16,16,1,1024]{3,1,2,0:T(8,128)(2,1)S(1)}, bf16[16,16,1,1024]{3,1,2,0:T(8,128)(2,1)}, u32[]{:S(2)}) copy-start(bf16[16,16,1,1024]{3,1,2,0:T(8,128)(2,1)} %param.11) | copy-start | bytes 1572868
  4.5 14.7 %collective-permute-start = (bf16[1,16,2,1024]{3,2,1,0:T(2,128)(2,1)S(1)}, bf16[1,16,2,1024]{3,2,1,0:T(2,128)(2,1)S(1)}, u32[]{:S(2)}, u32[]{:S(2)}) collective-permute-start(bf16[1,16,2,1024]{3,2,1,0:T(2,128)(2,1)S(1)} %get-tuple-element.75), channel_id=1, source_target_pairs={{0,16},{16,32},{32,48},{48,64},{64,80},{80,96},{96,112},{112,128},... | collective-permute-start | bytes 196616 | tf_op jit(solution)/shard_map/ppermute | solution.py:17
  9.6 9.6 %collective-permute-start.1 = (bf16[1,16,2,1024]{3,2,1,0:T(2,128)(2,1)S(1)}, bf16[1,16,2,1024]{3,2,1,0:T(2,128)(2,1)S(1)}, u32[]{:S(2)}, u32[]{:S(2)}) collective-permute-start(bf16[1,16,2,1024]{3,2,1,0:T(2,128)(2,1)S(1)} %get-tuple-element.76), channel_id=1, source_target_pairs={{16,0},{32,16},{48,32},{64,48},{80,64},{96,80},{112,96},{128,112},... | collective-permute-start | bytes 196616 | tf_op jit(solution)/shard_map/ppermute | solution.py:19
  15.5 18.9 %copy-start.13 = (f32[1024]{0:T(1024)}, f32[1024]{0:T(1024)S(1)}, u32[]{:S(2)}) copy-start(f32[1024]{0:T(1024)S(1)} %mul.642) | copy-start | bytes 12292
  15.6 18.9 %copy-start.15 = (f32[1024]{0:T(1024)}, f32[1024]{0:T(1024)S(1)}, u32[]{:S(2)}) copy-start(f32[1024]{0:T(1024)S(1)} %mul.714) | copy-start | bytes 12292
  15.7 18.8 %copy-start.17 = (f32[1024]{0:T(1024)}, f32[1024]{0:T(1024)S(1)}, u32[]{:S(2)}) copy-start(f32[1024]{0:T(1024)S(1)} %mul.711) | copy-start | bytes 12292
  15.7 18.7 %copy-start.19 = (f32[1024]{0:T(1024)}, f32[1024]{0:T(1024)S(1)}, u32[]{:S(2)}) copy-start(f32[1024]{0:T(1024)S(1)} %mul.708) | copy-start | bytes 12292
  15.8 18.7 %copy-start.21 = (f32[1024]{0:T(1024)}, f32[1024]{0:T(1024)S(1)}, u32[]{:S(2)}) copy-start(f32[1024]{0:T(1024)S(1)} %mul.705) | copy-start | bytes 12292
  15.9 18.6 %copy-start.23 = (f32[1024]{0:T(1024)}, f32[1024]{0:T(1024)S(1)}, u32[]{:S(2)}) copy-start(f32[1024]{0:T(1024)S(1)} %mul.702) | copy-start | bytes 12292
  16.0 18.5 %copy-start.25 = (f32[1024]{0:T(1024)}, f32[1024]{0:T(1024)S(1)}, u32[]{:S(2)}) copy-start(f32[1024]{0:T(1024)S(1)} %mul.699) | copy-start | bytes 12292
  16.0 18.5 %copy-start.27 = (f32[1024]{0:T(1024)}, f32[1024]{0:T(1024)S(1)}, u32[]{:S(2)}) copy-start(f32[1024]{0:T(1024)S(1)} %mul.696) | copy-start | bytes 12292
  16.1 18.4 %copy-start.29 = (f32[1024]{0:T(1024)}, f32[1024]{0:T(1024)S(1)}, u32[]{:S(2)}) copy-start(f32[1024]{0:T(1024)S(1)} %mul.693) | copy-start | bytes 12292
  16.2 18.3 %copy-start.31 = (f32[1024]{0:T(1024)}, f32[1024]{0:T(1024)S(1)}, u32[]{:S(2)}) copy-start(f32[1024]{0:T(1024)S(1)} %mul.690) | copy-start | bytes 12292
  16.3 18.3 %copy-start.33 = (f32[1024]{0:T(1024)}, f32[1024]{0:T(1024)S(1)}, u32[]{:S(2)}) copy-start(f32[1024]{0:T(1024)S(1)} %mul.687) | copy-start | bytes 12292
  16.4 18.2 %copy-start.35 = (f32[1024]{0:T(1024)}, f32[1024]{0:T(1024)S(1)}, u32[]{:S(2)}) copy-start(f32[1024]{0:T(1024)S(1)} %mul.684) | copy-start | bytes 12292
  16.4 18.1 %copy-start.37 = (f32[1024]{0:T(1024)}, f32[1024]{0:T(1024)S(1)}, u32[]{:S(2)}) copy-start(f32[1024]{0:T(1024)S(1)} %mul.681) | copy-start | bytes 12292
  16.5 18.1 %copy-start.39 = (f32[1024]{0:T(1024)}, f32[1024]{0:T(1024)S(1)}, u32[]{:S(2)}) copy-start(f32[1024]{0:T(1024)S(1)} %mul.678) | copy-start | bytes 12292
  16.6 18.0 %copy-start.41 = (f32[1024]{0:T(1024)}, f32[1024]{0:T(1024)S(1)}, u32[]{:S(2)}) copy-start(f32[1024]{0:T(1024)S(1)} %mul.675) | copy-start | bytes 12292
  16.7 17.9 %copy-start.43 = (f32[1024]{0:T(1024)}, f32[1024]{0:T(1024)S(1)}, u32[]{:S(2)}) copy-start(f32[1024]{0:T(1024)S(1)} %mul.672) | copy-start | bytes 12292
  16.7 17.9 %copy-start.45 = (f32[1024]{0:T(1024)}, f32[1024]{0:T(1024)S(1)}, u32[]{:S(2)}) copy-start(f32[1024]{0:T(1024)S(1)} %mul.669) | copy-start | bytes 12292
  16.8 17.8 %copy-start.47 = (f32[1024]{0:T(1024)}, f32[1024]{0:T(1024)S(1)}, u32[]{:S(2)}) copy-start(f32[1024]{0:T(1024)S(1)} %mul.666) | copy-start | bytes 12292
  16.9 17.7 %copy-start.49 = (f32[1024]{0:T(1024)}, f32[1024]{0:T(1024)S(1)}, u32[]{:S(2)}) copy-start(f32[1024]{0:T(1024)S(1)} %mul.663) | copy-start | bytes 12292
  19.4 5.4 %collective-permute-start.2 = (bf16[18,1,2,1024]{3,2,1,0:T(2,128)(2,1)S(1)}, bf16[18,1,2,1024]{3,2,1,0:T(2,128)(2,1)S(1)}, u32[]{:S(2)}, u32[]{:S(2)}) collective-permute-start(bf16[18,1,2,1024]{3,2,1,0:T(2,128)(2,1)S(1)} %get-tuple-element.71), channel_id=1, source_target_pairs={{0,1},{1,2},{2,3},{3,4},{4,5},{5,6},{6,7},{7,8},{8,9},{9,10},{10,1... | collective-permute-start | bytes 221192 | tf_op jit(solution)/shard_map/ppermute | solution.py:17
  22.7 5.1 %collective-permute-start.3 = (bf16[18,1,2,1024]{3,2,1,0:T(2,128)(2,1)S(1)}, bf16[18,1,2,1024]{3,2,1,0:T(2,128)(2,1)S(1)}, u32[]{:S(2)}, u32[]{:S(2)}) collective-permute-start(bf16[18,1,2,1024]{3,2,1,0:T(2,128)(2,1)S(1)} %get-tuple-element.72), channel_id=1, source_target_pairs={{1,0},{2,1},{3,2},{4,3},{5,4},{6,5},{7,6},{8,7},{9,8},{10,9},{11,1... | collective-permute-start | bytes 221192 | tf_op jit(solution)/shard_map/ppermute | solution.py:19
  59.6 12.8 %copy-start.2 = (f32[16,16,1,1024]{3,1,0,2:T(8,128)S(1)}, f32[16,16,1,1024]{3,1,0,2:T(8,128)}, u32[]{:S(2)}) copy-start(f32[16,16,1,1024]{3,1,0,2:T(8,128)} %get-tuple-element.33) | copy-start | bytes 3145732
  59.6 12.8 %copy-start.51 = (f32[1024]{0:T(1024)S(1)}, f32[1024]{0:T(1024)}, u32[]{:S(2)}) copy-start(f32[1024]{0:T(1024)} %mul.800) | copy-start | bytes 12292
  65.5 8.9 %collective-permute-start.4 = (bf16[1,16,2,1024]{3,2,1,0:T(2,128)(2,1)}, bf16[1,16,2,1024]{3,2,1,0:T(2,128)(2,1)}, u32[]{:S(2)}, u32[]{:S(2)}) collective-permute-start(bf16[1,16,2,1024]{3,2,1,0:T(2,128)(2,1)} %get-tuple-element.73), channel_id=1, source_target_pairs={{0,16},{16,32},{32,48},{48,64},{64,80},{80,96},{96,112},{112,128},... | collective-permute-start | bytes 196616 | tf_op jit(solution)/shard_map/ppermute | solution.py:17
  70.5 5.9 %collective-permute-start.5 = (bf16[1,16,2,1024]{3,2,1,0:T(2,128)(2,1)}, bf16[1,16,2,1024]{3,2,1,0:T(2,128)(2,1)}, u32[]{:S(2)}, u32[]{:S(2)}) collective-permute-start(bf16[1,16,2,1024]{3,2,1,0:T(2,128)(2,1)} %get-tuple-element.74), channel_id=1, source_target_pairs={{16,0},{32,16},{48,32},{64,48},{80,64},{96,80},{112,96},{128,112},... | collective-permute-start | bytes 196616 | tf_op jit(solution)/shard_map/ppermute | solution.py:19
  77.3 9.2 %collective-permute-start.6 = (bf16[18,1,2,1024]{3,2,1,0:T(2,128)(2,1)S(1)}, bf16[18,1,2,1024]{3,2,1,0:T(2,128)(2,1)S(1)}, u32[]{:S(2)}, u32[]{:S(2)}) collective-permute-start(bf16[18,1,2,1024]{3,2,1,0:T(2,128)(2,1)S(1)} %get-tuple-element.69), channel_id=1, source_target_pairs={{0,1},{1,2},{2,3},{3,4},{4,5},{5,6},{6,7},{7,8},{8,9},{9,10},{10,1... | collective-permute-start | bytes 221192 | tf_op jit(solution)/shard_map/ppermute | solution.py:17
  80.6 6.0 %collective-permute-start.7 = (bf16[18,1,2,1024]{3,2,1,0:T(2,128)(2,1)S(1)}, bf16[18,1,2,1024]{3,2,1,0:T(2,128)(2,1)S(1)}, u32[]{:S(2)}, u32[]{:S(2)}) collective-permute-start(bf16[18,1,2,1024]{3,2,1,0:T(2,128)(2,1)S(1)} %get-tuple-element.70), channel_id=1, source_target_pairs={{1,0},{2,1},{3,2},{4,3},{5,4},{6,5},{7,6},{8,7},{9,8},{10,9},{11,1... | collective-permute-start | bytes 221192 | tf_op jit(solution)/shard_map/ppermute | solution.py:19
  244.9 93.4 %copy-start.1 = (bf16[64,64]{1,0:T(8,128)(2,1)S(1)}, bf16[64,64]{1,0:T(8,128)(2,1)}, u32[]{:S(2)}) copy-start(bf16[64,64]{1,0:T(8,128)(2,1)} %param.10) | copy-start | bytes 24580
  (33 other events, 188.3 us)
where the time goes:
time: 344 us; the launch traced here: 339 us
  other arithmetic  105 us (31%)
  local copies, waits for them, and re-layouts  104 us (30%)
  blocking collectives  83.8 us (24%)
  starting transfers between devices  23.1 us (7%)
  matrix products  15.7 us (5%)
  waiting for transfers between devices  5.02 us (1%)
    psum x1, blocking collectives, shards(): lax.psum((grad_taps_part, grad_mix_part, grad_gain_part), ('gx', 'gy'))  83.8 us
    reshape x27, local copies, waits for them, and re-layouts, tap_grads(): rows_out.append(jnp.sum((shifted * grads).reshape(-1, channels), axis=0))  76.3 us
    reduce_sum x27, other arithmetic, tap_grads(): rows_out.append(jnp.sum((shifted * grads).reshape(-1, channels), axis=0))  57.9 us
    mul x4, other arithmetic, tap_grads(): rows_out.append(jnp.sum((shifted * grads).reshape(-1, channels), axis=0))  16.6 us
    ppermute x4, starting transfers between devices, extended_2(): lax.ppermute(tail, axis, [(i, (i + 1) % count) for i in range(ends)])  16.5 us
    dot_general x2, matrix products, slot_slabs(): jnp.einsum('xypf,skp->xyskf', level_pad, select.astype(jnp.bfloat16), pre...  9.5 us
    mul x1, other arithmetic, norm_forward(): mean_square = jnp.mean(depth_slots * depth_slots, axis=-1, keepdims=True)  9.4 us
    unnamed x1, other arithmetic  9.25 us
  transfers between devices with their start and end apart: 8, of which 2 were waited for; matrix products, arithmetic and copies ran while one was open for 4% of the time, Pallas kernels for 0%

commit v1 on v0

--- a/solution.py
+++ b/solution.py
@@ -161,8 +161,11 @@
     )
     grad_center = padded_grad[1:-1, 1:-1, :, channels:-channels].astype(jnp.float32)
     grad_taps_part = tap_grads(padded_in, grad_center, channels)
-    grad_taps, grad_mix, grad_gain = lax.psum(
-        (grad_taps_part, grad_mix_part, grad_gain_part), ("gx", "gy")
+    lift_loops_in = lambda payload, bus_axis, chip_axis: lax.psum(
+        lax.psum(payload, bus_axis), chip_axis
+    )
+    grad_taps, grad_mix, grad_gain = lift_loops_in(
+        (grad_taps_part, grad_mix_part, grad_gain_part), "gx", "gy"
     )
     return (mixed, grad_features, grad_taps, grad_gain, grad_mix)
 

time: 344 us -> 383 us (1.11)
  the two profiles are of different devices: /device:TPU:1 before, /device:TPU:128 now
where the time goes in v1:
time: 383 us; the launch traced here: 378 us
  blocking collectives  123 us (32%)
  other arithmetic  105 us (27%)
  local copies, waits for them, and re-layouts  104 us (27%)
  starting transfers between devices  23.4 us (6%)
  matrix products  15.7 us (4%)
  waiting for transfers between devices  4.64 us (1%)
    reshape x27, local copies, waits for them, and re-layouts, tap_grads(): rows_out.append(jnp.sum((shifted * grads).reshape(-1, channels), axis=0))  76.3 us
    psum x1, blocking collectives, shards(): lax.psum(lax.psum(payload, bus_axis), chip_axis)  74.8 us
    reduce_sum x27, other arithmetic, tap_grads(): rows_out.append(jnp.sum((shifted * grads).reshape(-1, channels), axis=0))  57.9 us
    psum x1, blocking collectives, shards(): lax.psum(payload, bus_axis)  48.1 us
    mul x4, other arithmetic, tap_grads(): rows_out.append(jnp.sum((shifted * grads).reshape(-1, channels), axis=0))  16.6 us
    ppermute x4, starting transfers between devices, extended_2(): lax.ppermute(head, axis, [((i + 1) % count, i) for i in range(ends)])  12.5 us
    ppermute x4, starting transfers between devices, extended_2(): lax.ppermute(tail, axis, [(i, (i + 1) % count) for i in range(ends)])  10.9 us
    dot_general x2, matrix products, slot_slabs(): jnp.einsum('xypf,skp->xyskf', level_pad, select.astype(jnp.bfloat16), pre...  9.5 us
  transfers between devices with their start and end apart: 8, of which 3 were waited for; matrix products, arithmetic and copies ran while one was open for 4% of the time, Pallas kernels for 0%

profile of v1, /device:TPU:128, one launch (start us, length us, event | category | flops | bytes accessed | tf_op | source)
XLA Modules:
  0.0 377.6 jit_solution(2375702078115320836)
XLA Ops:
  6.6 4.9 %collective-permute-start.1 = (bf16[1,16,2,1024]{3,2,1,0:T(2,128)(2,1)S(1)}, bf16[1,16,2,1024]{3,2,1,0:T(2,128)(2,1)S(1)}, u32[]{:S(2)}, u32[]{:S(2)}) collective-permute-start(bf16[1,16,2,1024]{3,2,1,0:T(2,128)(2,1)S(1)} %get-tuple-element.79), channel_id=1, source_target_pairs={{16,0},{32,16},{48,32},{64,48},{80,64},{96,80},{112,96},{128,112},... | collective-permute-start | bytes 196616 | tf_op jit(solution)/shard_map/ppermute | solution.py:19
  19.4 3.5 collective-permute-start.2
  25.0 4.1 %collective-permute-done.3 = bf16[18,1,2,1024]{3,2,1,0:T(2,128)(2,1)S(1)} collective-permute-done((bf16[18,1,2,1024]{3,2,1,0:T(2,128)(2,1)S(1)}, bf16[18,1,2,1024]{3,2,1,0:T(2,128)(2,1)S(1)}, u32[]{:S(2)}, u32[]{:S(2)}) %collective-permute-start.3) | collective-permute-done | bytes 73760 | tf_op jit(solution)/shard_map/ppermute | solution.py:19
  29.1 4.5 %convert_bitcast_fusion.1 = bf16[18,18,1,3,1024]{4,3,1,0,2:T(4,128)(2,1)S(1)} fusion(bf16[18,1,2,1024]{3,2,1,0:T(2,128)(2,1)S(1)} %collective-permute-done.3, bf16[18,1,2,1024]{3,2,1,0:T(2,128)(2,1)S(1)} %collective-permute-done.2, bf16[1,16,2,1024]{3,2,1,0:T(2,128)(2,1)S(1)} %collective-permute-done.1, bf16[16,16,2,1024]{3,2,1,0:T(2,128)(2,1)S(1)} %fusion.52, ...), kind=kOutput, calls=%fused_computation.88 | convolution fusion | flops 32845848 | bytes 3317773 | tf_op jit(solution)/shard_map/xypf,skp->xyskf/dot_general | solution.py:46
  36.0 9.4 %fusion.125 = (f32[16,16,1,1024]{3,1,0,2:T(8,128)}, f32[16,16,1,1024]{3,1,0,2:T(8,128)}) fusion(f32[1024]{0:T(1024)S(1)} %mul.720, bf16[18,18,1,64]{3,1,0,2:T(8,128)(2,1)S(1)} %get-tuple-element.108, bf16[18,18,1,1024]{3,1,0,2:T(8,128)(2,1)S(1)} %bitcast.278, f32[1024]{0:T(1024)S(1)} %mul.717, f32[1024]{0:T(1024)S(1)} %mul.714, ...), kind=kLoop, calls=%fused_computation.308 | loop fusion | flops 35389440 | bytes 8032256 | tf_op jit(solution)/shard_map/mul | solution.py:96
  54.1 3.1 multiply_convert_fusion.2
  68.7 4.9 %collective-permute-start.5 = (bf16[1,16,2,1024]{3,2,1,0:T(2,128)(2,1)}, bf16[1,16,2,1024]{3,2,1,0:T(2,128)(2,1)}, u32[]{:S(2)}, u32[]{:S(2)}) collective-permute-start(bf16[1,16,2,1024]{3,2,1,0:T(2,128)(2,1)} %get-tuple-element.77), channel_id=1, source_target_pairs={{16,0},{32,16},{48,32},{64,48},{80,64},{96,80},{112,96},{128,112},... | collective-permute-start | bytes 196616 | tf_op jit(solution)/shard_map/ppermute | solution.py:19
  76.7 3.5 collective-permute-start.6
  83.2 3.0 reshape.456
  86.4 5.0 %convert_bitcast_fusion = bf16[18,18,1,3,1024]{4,3,1,0,2:T(4,128)(2,1)S(1)} fusion(bf16[18,1,2,1024]{3,2,1,0:T(2,128)(2,1)S(1)} %collective-permute-done.7, bf16[18,1,2,1024]{3,2,1,0:T(2,128)(2,1)S(1)} %collective-permute-done.6, bf16[1,16,2,1024]{3,2,1,0:T(2,128)(2,1)} %collective-permute-done.5, bf16[16,16,2,1024]{3,2,1,0:T(2,128)(2,1)S(1)} %fusion.54, ...), kind=kOutput, calls=%fused_computation.87 | convolution fusion | flops 32845848 | bytes 3317773 | tf_op jit(solution)/shard_map/xypf,skp->xyskf/dot_general | solution.py:46
  93.6 4.0 %convert_multiply_fusion.2 = (f32[16,16,1,1024]{3,1,0,2:T(8,128)}, f32[16,16,1,1024]{3,1,0,2:T(8,128)}, f32[16,16,1,1024]{3,1,0,2:T(8,128)}, f32[16,16,1,1024]{3...) fusion(bf16[18,18,1,1024]{3,1,0,2:T(8,128)(2,1)S(1)} %bitcast.279, ...), kind=kLoop, calls=%fused_computation.2 | loop fusion | flops 8126464 | bytes 7520768 | tf_op jit(solution)/shard_map/mul | solution.py:91
  97.6 4.4 %convert_multiply_fusion.3 = (f32[16,16,1,1024]{3,1,0,2:T(8,128)}, f32[16,16,1,1024]{3,1,0,2:T(8,128)}, f32[16,16,1,1024]{3,1,0,2:T(8,128)}, f32[16,16,1,1024]{3...) fusion(bf16[18,18,1,64]{3,1,0,2:T(8,128)(2,1)S(1)} %copy-done.10, ...), kind=kLoop, calls=%fused_computation.3 | loop fusion | flops 8126464 | bytes 7562240 | tf_op jit(solution)/shard_map/mul | solution.py:91
  102.0 4.3 %convert_multiply_fusion = (f32[16,16,1,1024]{3,1,0,2:T(8,128)}, f32[16,16,1,1024]{3,1,0,2:T(8,128)}, f32[16,16,1,1024]{3,1,0,2:T(8,128)}, f32[16,16,1,1024]{3,1...) fusion(bf16[18,18,1,64]{3,1,0,2:T(8,128)(2,1)S(1)} %copy-done.10, ...), kind=kLoop, calls=%fused_computation | loop fusion | flops 8126464 | bytes 7520768 | tf_op jit(solution)/shard_map/mul | solution.py:91
  106.3 4.0 %convert_multiply_fusion.1 = (f32[16,16,1,1024]{3,1,0,2:T(8,128)}, f32[16,16,1,1024]{3,1,0,2:T(8,128)}, f32[16,16,1,1024]{3,1,0,2:T(8,128)}, f32[16,16,1,1024]{3...) fusion(bf16[18,18,1,1024]{3,1,0,2:T(8,128)(2,1)S(1)} %bitcast.2, ...), kind=kLoop, calls=%fused_computation.1 | loop fusion | flops 4980736 | bytes 14680064 | tf_op jit(solution)/shard_map/mul | solution.py:91
  110.3 2.9 reshape.482
  115.3 2.8 reshape.458
  120.3 3.0 reshape.461
  125.5 2.8 reshape.464
  130.5 2.8 reshape.467
  135.5 2.8 reshape.470
  145.5 2.8 reshape.475
  150.5 2.8 reshape.478
  155.4 2.8 reshape.476
  160.4 2.8 reshape.473
  165.4 2.8 reshape.479
  180.4 2.8 reshape.463
  185.4 3.1 reshape.466
  200.6 2.8 reshape.483
  205.6 2.8 reshape.480
  245.0 9.3 %fusion.106 = bf16[16,16,1,1024]{3,1,2,0:T(8,128)(2,1)} fusion(f32[]{:T(128)S(6)} %convert_element_type.307, f32[1024]{0:T(1024)S(1)} %copy-done.14, bf16[18,18,1,64]{3,1,0,2:T(8,128)(2,1)S(1)} %bitcast.290, bf16[18,18,1,1024]{3,1,0,2:T(8,128)(2,1)S(1)} %bitcast.287, f32[1024]{0:T(1024)S(1)} %mul.645, f32[1024]{0:T(1024)S(1)} %mul.648, ...), kind=kLoop, calls=%fused_computation.245 | loop fusion | flops 36175872 | bytes 6983684
  254.4 48.1 %all-reduce.4 = (f32[27,64]{1,0:T(8,128)S(1)}, f32[64]{0:T(128)S(1)}, f32[64,64]{1,0:T(8,128)S(1)}) all-reduce(f32[27,64]{1,0:T(8,128)S(1)} %stack.111, f32[64]{0:T(128)S(1)} %copy-done.54, f32[64,64]{1,0:T(8,128)S(1)} %convolution_bitcast_fusion), channel_id=1, replica_groups=mesh['gx'=16,'gy'=16] {'gx'}, use_global_device_ids=true, to_apply=%region_31.32 | all-reduce | flops 5888 | bytes 47104 | tf_op jit(solution)/shard_map/psum | solution.py:165
  302.5 74.8 %all-reduce.3 = (f32[27,64]{1,0:T(8,128)}, f32[64]{0:T(128)}, f32[64,64]{1,0:T(8,128)}) all-reduce(f32[27,64]{1,0:T(8,128)S(1)} %get-tuple-element.32, f32[64]{0:T(128)S(1)} %get-tuple-element.33, f32[64,64]{1,0:T(8,128)S(1)} %get-tuple-element.34), channel_id=1, replica_groups=mesh['gx'=16,'gy'=16] {'gy'}, use_global_device_ids=true, to_apply=%region_32.33 | all-reduce | flops 5888 | bytes 47104 | tf_op jit(solution)/shard_map/psum | solution.py:164
  (259 shorter events, 137.4 us)
Async XLA Ops:
  0.6 53.5 %copy-start = (bf16[64,64]{1,0:T(8,128)(2,1)S(1)}, bf16[64,64]{1,0:T(8,128)(2,1)}, u32[]{:S(2)}) copy-start(bf16[64,64]{1,0:T(8,128)(2,1)} %param.10) | copy-start | bytes 24580
  4.4 12.4 %copy-start.7 = (bf16[16,16,1,1024]{3,1,2,0:T(8,128)(2,1)S(1)}, bf16[16,16,1,1024]{3,1,2,0:T(8,128)(2,1)}, u32[]{:S(2)}) copy-start(bf16[16,16,1,1024]{3,1,2,0:T(8,128)(2,1)} %param.11) | copy-start | bytes 1572868
  4.5 14.6 %collective-permute-start = (bf16[1,16,2,1024]{3,2,1,0:T(2,128)(2,1)S(1)}, bf16[1,16,2,1024]{3,2,1,0:T(2,128)(2,1)S(1)}, u32[]{:S(2)}, u32[]{:S(2)}) collective-permute-start(bf16[1,16,2,1024]{3,2,1,0:T(2,128)(2,1)S(1)} %get-tuple-element.78), channel_id=1, source_target_pairs={{0,16},{16,32},{32,48},{48,64},{64,80},{80,96},{96,112},{112,128},... | collective-permute-start | bytes 196616 | tf_op jit(solution)/shard_map/ppermute | solution.py:17
  6.6 12.6 %collective-permute-start.1 = (bf16[1,16,2,1024]{3,2,1,0:T(2,128)(2,1)S(1)}, bf16[1,16,2,1024]{3,2,1,0:T(2,128)(2,1)S(1)}, u32[]{:S(2)}, u32[]{:S(2)}) collective-permute-start(bf16[1,16,2,1024]{3,2,1,0:T(2,128)(2,1)S(1)} %get-tuple-element.79), channel_id=1, source_target_pairs={{16,0},{32,16},{48,32},{64,48},{80,64},{96,80},{112,96},{128,112},... | collective-permute-start | bytes 196616 | tf_op jit(solution)/shard_map/ppermute | solution.py:19
  15.4 20.4 %copy-start.13 = (f32[1024]{0:T(1024)}, f32[1024]{0:T(1024)S(1)}, u32[]{:S(2)}) copy-start(f32[1024]{0:T(1024)S(1)} %mul.642) | copy-start | bytes 12292
  15.5 20.3 %copy-start.15 = (f32[1024]{0:T(1024)}, f32[1024]{0:T(1024)S(1)}, u32[]{:S(2)}) copy-start(f32[1024]{0:T(1024)S(1)} %mul.714) | copy-start | bytes 12292
  15.6 20.2 %copy-start.17 = (f32[1024]{0:T(1024)}, f32[1024]{0:T(1024)S(1)}, u32[]{:S(2)}) copy-start(f32[1024]{0:T(1024)S(1)} %mul.711) | copy-start | bytes 12292
  15.6 20.2 %copy-start.19 = (f32[1024]{0:T(1024)}, f32[1024]{0:T(1024)S(1)}, u32[]{:S(2)}) copy-start(f32[1024]{0:T(1024)S(1)} %mul.708) | copy-start | bytes 12292
  15.7 20.1 %copy-start.21 = (f32[1024]{0:T(1024)}, f32[1024]{0:T(1024)S(1)}, u32[]{:S(2)}) copy-start(f32[1024]{0:T(1024)S(1)} %mul.705) | copy-start | bytes 12292
  15.8 20.0 %copy-start.23 = (f32[1024]{0:T(1024)}, f32[1024]{0:T(1024)S(1)}, u32[]{:S(2)}) copy-start(f32[1024]{0:T(1024)S(1)} %mul.702) | copy-start | bytes 12292
  15.9 20.0 %copy-start.25 = (f32[1024]{0:T(1024)}, f32[1024]{0:T(1024)S(1)}, u32[]{:S(2)}) copy-start(f32[1024]{0:T(1024)S(1)} %mul.699) | copy-start | bytes 12292
  16.0 19.9 %copy-start.27 = (f32[1024]{0:T(1024)}, f32[1024]{0:T(1024)S(1)}, u32[]{:S(2)}) copy-start(f32[1024]{0:T(1024)S(1)} %mul.696) | copy-start | bytes 12292
  16.0 19.8 %copy-start.29 = (f32[1024]{0:T(1024)}, f32[1024]{0:T(1024)S(1)}, u32[]{:S(2)}) copy-start(f32[1024]{0:T(1024)S(1)} %mul.693) | copy-start | bytes 12292
  16.1 19.8 %copy-start.31 = (f32[1024]{0:T(1024)}, f32[1024]{0:T(1024)S(1)}, u32[]{:S(2)}) copy-start(f32[1024]{0:T(1024)S(1)} %mul.690) | copy-start | bytes 12292
  16.2 19.7 %copy-start.33 = (f32[1024]{0:T(1024)}, f32[1024]{0:T(1024)S(1)}, u32[]{:S(2)}) copy-start(f32[1024]{0:T(1024)S(1)} %mul.687) | copy-start | bytes 12292
  16.3 19.6 %copy-start.35 = (f32[1024]{0:T(1024)}, f32[1024]{0:T(1024)S(1)}, u32[]{:S(2)}) copy-start(f32[1024]{0:T(1024)S(1)} %mul.684) | copy-start | bytes 12292
  16.3 19.6 %copy-start.37 = (f32[1024]{0:T(1024)}, f32[1024]{0:T(1024)S(1)}, u32[]{:S(2)}) copy-start(f32[1024]{0:T(1024)S(1)} %mul.681) | copy-start | bytes 12292
  16.4 19.5 %copy-start.39 = (f32[1024]{0:T(1024)}, f32[1024]{0:T(1024)S(1)}, u32[]{:S(2)}) copy-start(f32[1024]{0:T(1024)S(1)} %mul.678) | copy-start | bytes 12292
  16.5 19.4 %copy-start.41 = (f32[1024]{0:T(1024)}, f32[1024]{0:T(1024)S(1)}, u32[]{:S(2)}) copy-start(f32[1024]{0:T(1024)S(1)} %mul.675) | copy-start | bytes 12292
  16.6 19.4 %copy-start.43 = (f32[1024]{0:T(1024)}, f32[1024]{0:T(1024)S(1)}, u32[]{:S(2)}) copy-start(f32[1024]{0:T(1024)S(1)} %mul.672) | copy-start | bytes 12292
  16.7 19.3 %copy-start.45 = (f32[1024]{0:T(1024)}, f32[1024]{0:T(1024)S(1)}, u32[]{:S(2)}) copy-start(f32[1024]{0:T(1024)S(1)} %mul.669) | copy-start | bytes 12292
  16.7 19.2 %copy-start.47 = (f32[1024]{0:T(1024)}, f32[1024]{0:T(1024)S(1)}, u32[]{:S(2)}) copy-start(f32[1024]{0:T(1024)S(1)} %mul.666) | copy-start | bytes 12292
  16.8 19.2 %copy-start.49 = (f32[1024]{0:T(1024)}, f32[1024]{0:T(1024)S(1)}, u32[]{:S(2)}) copy-start(f32[1024]{0:T(1024)S(1)} %mul.663) | copy-start | bytes 12292
  19.4 5.6 %collective-permute-start.2 = (bf16[18,1,2,1024]{3,2,1,0:T(2,128)(2,1)S(1)}, bf16[18,1,2,1024]{3,2,1,0:T(2,128)(2,1)S(1)}, u32[]{:S(2)}, u32[]{:S(2)}) collective-permute-start(bf16[18,1,2,1024]{3,2,1,0:T(2,128)(2,1)S(1)} %get-tuple-element.74), channel_id=1, source_target_pairs={{0,1},{1,2},{2,3},{3,4},{4,5},{5,6},{6,7},{7,8},{8,9},{9,10},{10,1... | collective-permute-start | bytes 221192 | tf_op jit(solution)/shard_map/ppermute | solution.py:17
  22.9 6.2 %collective-permute-start.3 = (bf16[18,1,2,1024]{3,2,1,0:T(2,128)(2,1)S(1)}, bf16[18,1,2,1024]{3,2,1,0:T(2,128)(2,1)S(1)}, u32[]{:S(2)}, u32[]{:S(2)}) collective-permute-start(bf16[18,1,2,1024]{3,2,1,0:T(2,128)(2,1)S(1)} %get-tuple-element.75), channel_id=1, source_target_pairs={{1,0},{2,1},{3,2},{4,3},{5,4},{6,5},{7,6},{8,7},{9,8},{10,9},{11,1... | collective-permute-start | bytes 221192 | tf_op jit(solution)/shard_map/ppermute | solution.py:19
  61.0 12.6 %copy-start.2 = (f32[16,16,1,1024]{3,1,0,2:T(8,128)S(1)}, f32[16,16,1,1024]{3,1,0,2:T(8,128)}, u32[]{:S(2)}) copy-start(f32[16,16,1,1024]{3,1,0,2:T(8,128)} %get-tuple-element.36) | copy-start | bytes 3145732
  61.0 12.6 %copy-start.51 = (f32[1024]{0:T(1024)S(1)}, f32[1024]{0:T(1024)}, u32[]{:S(2)}) copy-start(f32[1024]{0:T(1024)} %mul.800) | copy-start | bytes 12292
  66.8 8.7 %collective-permute-start.4 = (bf16[1,16,2,1024]{3,2,1,0:T(2,128)(2,1)}, bf16[1,16,2,1024]{3,2,1,0:T(2,128)(2,1)}, u32[]{:S(2)}, u32[]{:S(2)}) collective-permute-start(bf16[1,16,2,1024]{3,2,1,0:T(2,128)(2,1)} %get-tuple-element.76), channel_id=1, source_target_pairs={{0,16},{16,32},{32,48},{48,64},{64,80},{80,96},{96,112},{112,128},... | collective-permute-start | bytes 196616 | tf_op jit(solution)/shard_map/ppermute | solution.py:17
  68.7 7.1 %collective-permute-start.5 = (bf16[1,16,2,1024]{3,2,1,0:T(2,128)(2,1)}, bf16[1,16,2,1024]{3,2,1,0:T(2,128)(2,1)}, u32[]{:S(2)}, u32[]{:S(2)}) collective-permute-start(bf16[1,16,2,1024]{3,2,1,0:T(2,128)(2,1)} %get-tuple-element.77), channel_id=1, source_target_pairs={{16,0},{32,16},{48,32},{64,48},{80,64},{96,80},{112,96},{128,112},... | collective-permute-start | bytes 196616 | tf_op jit(solution)/shard_map/ppermute | solution.py:19
  76.7 9.5 %collective-permute-start.6 = (bf16[18,1,2,1024]{3,2,1,0:T(2,128)(2,1)S(1)}, bf16[18,1,2,1024]{3,2,1,0:T(2,128)(2,1)S(1)}, u32[]{:S(2)}, u32[]{:S(2)}) collective-permute-start(bf16[18,1,2,1024]{3,2,1,0:T(2,128)(2,1)S(1)} %get-tuple-element.72), channel_id=1, source_target_pairs={{0,1},{1,2},{2,3},{3,4},{4,5},{5,6},{6,7},{7,8},{8,9},{9,10},{10,1... | collective-permute-start | bytes 221192 | tf_op jit(solution)/shard_map/ppermute | solution.py:17
  80.2 6.2 %collective-permute-start.7 = (bf16[18,1,2,1024]{3,2,1,0:T(2,128)(2,1)S(1)}, bf16[18,1,2,1024]{3,2,1,0:T(2,128)(2,1)S(1)}, u32[]{:S(2)}, u32[]{:S(2)}) collective-permute-start(bf16[18,1,2,1024]{3,2,1,0:T(2,128)(2,1)S(1)} %get-tuple-element.73), channel_id=1, source_target_pairs={{1,0},{2,1},{3,2},{4,3},{5,4},{6,5},{7,6},{8,7},{9,8},{10,9},{11,1... | collective-permute-start | bytes 221192 | tf_op jit(solution)/shard_map/ppermute | solution.py:19
  244.8 132.5 %copy-start.1 = (bf16[64,64]{1,0:T(8,128)(2,1)S(1)}, bf16[64,64]{1,0:T(8,128)(2,1)}, u32[]{:S(2)}) copy-start(bf16[64,64]{1,0:T(8,128)(2,1)} %param.10) | copy-start | bytes 24580
  (33 other events, 187.8 us)
